TPU v7x, 256 devices: a whole 4x4x8 slice. The times are simulated.
256 devices in a mesh: vocab: 64 (over y, z, core), hidden: 4 (over x).
Axes of the slice: x: 4, y: 4, z: 8, core: 2. Of those that a mesh axis runs over, the one named last changes fastest.
Arguments:
- states: bfloat16 [1024, 7168], P(('vocab', 'hidden')), may hold values from -32 to 32
- head: bfloat16 [7168, 129280], P('hidden', 'vocab'), may hold values from -1 to 1
Outputs:
- logp: float32 [1024, 129280], P('hidden', 'vocab')
All inputs are finite; a program needn't handle non-finite values.
Results may differ from a plain program's by a relative error of at most 0.0003.
Values may be sent and summed in bfloat16 or wider, within the bound.
A program may use at most 128 MiB of HBM per device.

v0:
```python
import math

import jax
import jax.numpy as jnp
from jax import lax
from jax.sharding import Mesh
from jax.sharding import PartitionSpec as P

VOCAB = ("vocab_0", "vocab_1", "vocab_2")
VOCAB_HIDDEN = ("vocab_0", "vocab_1", "vocab_2", "hidden")


sharpness = 4.0
minp_offset = math.log(10.0)
logp_floor = 30.0


def joined_along(pieces, dim):
    pieces = jnp.moveaxis(pieces, 0, dim)
    dims = pieces.shape
    return pieces.reshape(*dims[:dim], dims[dim] * dims[dim + 1], *dims[dim + 2 :])


def gather_in_order(shard, axes, order):
    pieces = shard
    for k in order:
        pieces = lax.all_gather(pieces, axes[k])
    done = order[::-1]
    back = [done.index(k) for k in range(len(axes))]
    pieces = pieces.transpose(*back, *range(len(axes), pieces.ndim))
    return pieces.reshape(-1, *shard.shape)


def gather_axes(shard, axes, order, dim):
    return joined_along(gather_in_order(shard, axes, order), dim)


def from_everyone(shard, axis):
    devices = lax.axis_size(axis)
    return lax.all_to_all(
        jnp.broadcast_to(shard[None], (devices, *shard.shape)), axis, 0, 0, tiled=True
    )


def over_copies(shard, axis):
    return from_everyone(shard, axis).max(axis=0)


def over_copies_2(shard, axis):
    return from_everyone(shard, axis).sum(axis=0)


def filtered(logits, top):
    shifted = logits - top[:, None]
    return shifted + jax.nn.log_sigmoid(sharpness * (shifted + minp_offset))


def body(states, head):
    slices = lax.all_to_all(states, "hidden", split_axis=1, concat_axis=0, tiled=True)
    gathered = gather_axes(slices, VOCAB, (0, 1, 2), 0)
    logits = lax.psum_scatter(
        jnp.dot(gathered, head, preferred_element_type=jnp.float32),
        "hidden",
        scatter_dimension=0,
        tiled=True,
    )
    top = over_copies(jnp.max(logits, axis=1), VOCAB)
    gated = filtered(logits, top)
    total = over_copies_2(jnp.sum(jnp.exp(gated), axis=1), VOCAB)
    return jnp.maximum(gated - jnp.log(total)[:, None], -logp_floor)


def solution(mesh):
    torus = Mesh(
        mesh.devices.reshape(4, 8, 2, mesh.shape["hidden"]),
        ("vocab_0", "vocab_1", "vocab_2", "hidden"),
    )
    return jax.shard_map(
        body,
        mesh=torus,
        in_specs=(P(VOCAB_HIDDEN, None), P("hidden", VOCAB)),
        out_specs=P("hidden", VOCAB),
        check_vma=False,
    )
```

profile of v0, /device:TPU:1, one launch (start us, length us, event | category | flops | bytes accessed | tf_op | source)
XLA Modules:
  0.0 236.1 jit_solution(12771082451407229781)
XLA Ops:
  6.5 0.0 all-gather.5.cloned.1.call-start
  6.5 9.3 %all_to_all.28 = bf16[4,4,1792]{2,0,1:T(4,128)(2,1)S(1)} all-to-all(bf16[4,4,1792]{2,0,1:T(4,128)(2,1)} %bitcast.13), channel_id=1, replica_groups=mesh['vocab_0'=4,'vocab_1'=8,'vocab_2'=2,'hidden'=4] {'hidden'}, dimensions={1} | all-to-all | bytes 114688 | tf_op jit(solution)/shard_map/all_to_all | solution.py:59
  15.8 10.6 %all_gather.19 = bf16[4,16,1792]{2,1,0:T(8,128)(2,1)} all-gather(bf16[1,16,1792]{2,1,0:T(8,128)(2,1)S(1)} %all_gather.18), channel_id=1, replica_groups=mesh['vocab_0'=4,'vocab_1'=8,'vocab_2'=2,'hidden'=4] {'vocab_0'}, dimensions={0}, use_global_device_ids=true | all-gather | bytes 286720 | tf_op jit(solution)/shard_map/all_gather | solution.py:27
  26.4 0.0 all-gather.5.cloned.1.call-update
  26.4 0.0 all-gather.7.cloned.1.call-start
  26.5 41.7 %all-gather.5.cloned.1.call-done = bf16[32,16,1792]{2,1,0:T(8,128)(2,1)} async-done(((bf16[4,16,1792]{2,1,0:T(8,128)(2,1)}), bf16[32,16,1792]{2,1,0:T(8,128)(2,1)}) %all-gather.5.cloned.1.call-update) | async-done | bytes 1835024 | tf_op jit(solution)/shard_map/all_gather | solution.py:27
  68.2 0.0 all-gather.7.cloned.1.call-update
  68.2 0.0 reduce-scatter.2.cloned.1.call-start
  68.3 23.0 %all-gather.7.cloned.1.call-done = bf16[16,4,16,1792]{3,2,1,0:T(8,128)(2,1)} async-done(((bf16[8,4,16,1792]{3,2,1,0:T(8,128)(2,1)}), bf16[16,4,16,1792]{3,2,1,0:T(8,128)(2,1)}) %all-gather.7.cloned.1.call-update) | async-done | bytes 3670032 | tf_op jit(solution)/shard_map/all_gather | solution.py:27
  91.3 0.0 copy-start.1
  91.3 2.6 %copy.11 = bf16[4,8,2,16,1792]{4,3,2,1,0:T(8,128)(2,1)S(1)} copy(bf16[4,8,2,16,1792]{4,3,0,1,2:T(8,128)(2,1)} %bitcast.9) | data formatting | bytes 7340032 | tf_op jit(solution)/shard_map/transpose | solution.py:30
  93.9 1.6 copy-done.1
  95.4 10.3 %fusion.2 = f32[1024,2020]{0,1:T(8,128)} fusion(bf16[1024,1792]{1,0:T(8,128)(2,1)S(1)} %bitcast.10, bf16[1792,2020]{0,1:T(8,128)(2,1)S(1)} %copy-done.1), kind=kOutput, calls=%fused_computation.5 | convolution fusion | flops 7413432320 | bytes 19183616 | tf_op jit(solution)/shard_map/dot_general | solution.py:62
  105.7 0.0 reduce-scatter.2.cloned.1.call-update
  105.7 83.2 %reduce-scatter.2.cloned.1.call-done = f32[256,2020]{0,1:T(8,128)} async-done(((f32[1024,2020]{0,1:T(8,128)}), f32[256,2020]{0,1:T(8,128)}) %reduce-scatter.2.cloned.1.call-update) | async-done | bytes 2068496 | tf_op jit(solution)/shard_map/reduce_scatter | solution.py:61
  188.9 0.0 copy-start
  188.9 2.0 reduce_max.18
  191.0 20.2 %all_to_all.29 = f32[64,1,256]{2,1,0:T(1,128)S(1)} all-to-all(f32[64,1,256]{2,1,0:T(1,128)S(1)} %broadcast_in_dim.4), channel_id=1, replica_groups=mesh['vocab_0'=4,'vocab_1'=8,'vocab_2'=2,'hidden'=4] {'vocab_0','vocab_1..., dimensions={0} | all-to-all | bytes 131072 | tf_op jit(solution)/shard_map/all_to_all | solution.py:40
  211.2 0.1 reduce_max.19
  211.3 0.0 copy-done
  211.3 1.6 exponential_reduce_fusion
  213.0 13.6 %all_to_all.30 = f32[64,1,256]{2,1,0:T(1,128)S(1)} all-to-all(f32[64,1,256]{2,1,0:T(1,128)S(1)} %broadcast_in_dim.5), channel_id=1, replica_groups=mesh['vocab_0'=4,'vocab_1'=8,'vocab_2'=2,'hidden'=4] {'vocab_0','vocab_1..., dimensions={0} | all-to-all | bytes 131072 | tf_op jit(solution)/shard_map/all_to_all | solution.py:40
  226.6 0.1 reduce_sum.19
  226.7 2.9 %subtract_maximum_fusion = f32[256,2020]{0,1:T(8,128)} fusion(f32[256]{0:T(256)S(1)} %log.7, f32[256,2020]{0,1:T(8,128)S(1)} %copy-done, f32[256]{0:T(256)S(1)} %reduce_max.19), kind=kLoop, calls=%fused_computation.3 | loop fusion | flops 7239680 | bytes 4139008 | tf_op jit(solution)/shard_map/max | solution.py:70
  (4 shorter events, 0.1 us)
Async XLA Ops:
  6.5 61.7 %all-gather.5.cloned.1.call-start = ((), (), s32[]{:S(2)}) async-start(), calls=%async_computation.5 | async-start | bytes 2064384 | tf_op jit(solution)/shard_map/all_gather | solution.py:27
  26.4 64.9 %all-gather.7.cloned.1.call-start = ((), (), s32[]{:S(2)}) async-start(), calls=%async_computation.6 | async-start | bytes 5505024 | tf_op jit(solution)/shard_map/all_gather | solution.py:27
  68.2 120.7 %reduce-scatter.2.cloned.1.call-start = ((), (), s32[]{:S(2)}) async-start(), calls=%async_computation.4 | async-start | bytes 10362880 | tf_op jit(solution)/shard_map/reduce_scatter | solution.py:61
  91.3 4.2 %copy-start.1 = (bf16[1792,2020]{0,1:T(8,128)(2,1)S(1)}, bf16[1792,2020]{0,1:T(8,128)(2,1)}, u32[]{:S(2)}) copy-start(bf16[1792,2020]{0,1:T(8,128)(2,1)} %param.3) | copy-start | bytes 21719044
  188.9 22.4 %copy-start = (f32[256,2020]{0,1:T(8,128)S(1)}, f32[256,2020]{0,1:T(8,128)}, u32[]{:S(2)}) copy-start(f32[256,2020]{0,1:T(8,128)} %reduce-scatter.2.cloned.1.call-done) | copy-start | bytes 6205444
Sparse Core Ops, SparseCore 0:
  26.5 41.6 all-gather.4
  70.0 21.2 all-gather.6
  105.9 82.9 reduce-scatter.1
where the time goes:
time: 236 us
  waiting for transfers between devices  148 us (63%)
  blocking collectives  53.7 us (23%)
  between operations  13.1 us (6%)
  matrix products  10.3 us (4%)
  other arithmetic  6.69 us (3%)
  local copies, waits for them, and re-layouts  4.26 us (2%)
    reduce_scatter x1, waiting for transfers between devices, body(): lax.psum_scatter(jnp.dot(gathered, head, preferred_element_type=jnp.float...  83.2 us
    all_gather x2, waiting for transfers between devices, gather_in_order(): pieces = lax.all_gather(pieces, axes[k])  64.7 us
    all_to_all x2, blocking collectives, from_everyone(): lax.all_to_all(jnp.broadcast_to(shard[None], (devices, *shard.shape)), ax...  33.9 us
    all_gather x1, blocking collectives, gather_in_order(): pieces = lax.all_gather(pieces, axes[k])  10.6 us
    dot_general x1, matrix products, body(): jnp.dot(gathered, head, preferred_element_type=jnp.float32)  10.3 us
    all_to_all x1, blocking collectives, body(): lax.all_to_all(states, 'hidden', split_axis=1, concat_axis=0, tiled=True)  9.27 us
  transfers between devices with their start and end apart: 3, of which 3 were waited for; matrix products, arithmetic and copies ran while one was open for 0% of the time, Pallas kernels for 0%

commit v1 on v0

v1 whole, which is shorter than its diff:
```python
import functools
import math

import jax
import jax.numpy as jnp
from jax import lax
from jax.experimental import pallas as pl
from jax.experimental.pallas import tpu as pltpu
from jax.sharding import Mesh
from jax.sharding import PartitionSpec as P

MESH = pl.DeviceIdType.MESH
VOCAB = ("y", "z", "c")
VOCAB_HIDDEN = ("y", "z", "c", "x")
NX, NY, NZ, NC = 4, 4, 8, 2

sharpness = 4.0
minp_offset = math.log(10.0)
logp_floor = 30.0

BLOCK = 128
HALF = 64
PIECE = 16
LOCAL = 4
DEPTH = 1792
COLS = 2020
CHUNKS = ((0, 512), (512, 512), (1024, 512), (1536, 484))
POWER = 7


def coded(v):
    v2 = v * v
    v3 = v2 * v
    return (v3 * (v2 * v2)).astype(jnp.bfloat16)


def decoded(w):
    w = w.astype(jnp.float32)
    r = jnp.exp2(jnp.log2(jnp.abs(w)) * (1.0 / POWER))
    return jnp.where(w < 0.0, -r, r)


def kernel(
    states, head, gated_out, lnt_out,
    weights, xin, st, prod, s1out, s1in, s2out, s2in, acc, col, ex1, ex2,
    w_sem, xl_sem, xs_sem, xr_sem, ys_sem, yr_sem, zs_sem, zr_sem, cs_sem, cr_sem,
    s1s_sem, s1r_sem, s2s_sem, s2r_sem, e1s_sem, e1r_sem, e2s_sem, e2r_sem, o_sem,
):
    x, y, z, c = (lax.axis_index(n) for n in ("x", "y", "z", "c"))
    q = y * NC + c

    def at(axis, index):
        here = {"x": x, "y": y, "z": z, "c": c}
        here[axis] = index
        return (here["y"], here["z"], here["c"], here["x"])

    def in_plane(index):
        return (index // NC, z, index % NC, x)

    def remote(src, dst, send, recv, device):
        return pltpu.make_async_remote_copy(
            src_ref=src, dst_ref=dst, send_sem=send, recv_sem=recv,
            device_id=device, device_id_type=MESH,
        )

    w_copies = [
        pltpu.make_async_copy(
            head.at[pl.ds(256 * k, 256), :], weights.at[pl.ds(256 * k, 256), :], w_sem.at[k]
        )
        for k in range(7)
    ]
    for copy in w_copies:
        copy.start()
    own_piece = pltpu.make_async_copy(
        states.at[:, pl.ds(pl.multiple_of(x * DEPTH, 128), DEPTH)], xin.at[x], xl_sem
    )
    own_piece.start()

    barrier = pltpu.get_barrier_semaphore()
    partners = [at("x", (x + k) % NX) for k in range(1, NX)]
    partners += [in_plane((q + k) % (NY * NC)) for k in range(1, NY * NC)]
    partners += [at("z", (z + k) % NZ) for k in range(1, NZ)]
    for device in partners:
        pl.semaphore_signal(barrier, inc=1, device_id=device, device_id_type=MESH)
    pl.semaphore_wait(barrier, len(partners))

    x_copies = []
    for k in range(1, NX):
        to = (x + k) % NX
        x_copies.append(remote(
            states.at[:, pl.ds(pl.multiple_of(to * DEPTH, 128), DEPTH)], xin.at[x],
            xs_sem.at[k - 1], xr_sem.at[k - 1], at("x", to),
        ))
        x_copies[-1].start()
    own_piece.wait()
    for copy in x_copies:
        copy.wait_recv()
    mine = pl.multiple_of(c * HALF + y * PIECE, PIECE)
    pieces = [xin[k].astype(jnp.float32) for k in range(NX)]
    st[z, pl.ds(mine, PIECE), :] = jnp.concatenate(pieces, axis=0).astype(jnp.bfloat16)

    y_copies = []
    for k in range(1, NY):
        here = st.at[z, pl.ds(mine, PIECE), :]
        y_copies.append(remote(
            here, here, ys_sem.at[k - 1], yr_sem.at[k - 1], at("y", (y + k) % NY)
        ))
        y_copies[-1].start()
    for copy in y_copies:
        copy.wait_recv()

    half = pl.multiple_of(c * HALF, HALF)

    def along_z(direction, step, block, rows, count):
        there = st.at[block, pl.ds(rows, count), :]
        to = (z + 1) % NZ if direction == 0 else (z + NZ - 1) % NZ
        return remote(
            there, there, zs_sem.at[direction, step], zr_sem.at[direction, step], at("z", to)
        )

    def to_sibling(b, block):
        there = st.at[block, pl.ds(half, HALF), :]
        return remote(there, there, cs_sem.at[b], cr_sem.at[b], at("c", 1 - c))

    along_z(0, 1, z, half, HALF).start()
    along_z(1, 1, z, half, HALF).start()
    to_sibling(0, z).start()
    for copy in w_copies:
        copy.wait()

    right, left, across = (x + 1) % NX, (x + NX - 1) % NX, (x + 2) % NX

    def first_hop(b, h):
        return remote(
            s1out.at[b, h], s1in.at[b, h], s1s_sem.at[b, h], s1r_sem.at[b, h],
            at("x", right if h == 0 else left),
        )

    def second_hop(b, h):
        return remote(
            s2out.at[b, h], s2in.at[b, h], s2s_sem.at[b, h], s2r_sem.at[b, h],
            at("x", right if h == 0 else left),
        )

    def rows_for(h, d):
        return pl.ds(pl.multiple_of(h * HALF + d * PIECE, PIECE), PIECE)

    def block_at(b):
        s = (b + 1) // 2
        return (z + s * (1 - 2 * (b % 2)) + NZ) % NZ

    def step(b, carry):
        for s in (1, 2, 3):
            @pl.when(b == 2 * s - 1)
            def _():
                behind, ahead = (z + NZ - s) % NZ, (z + s) % NZ
                for direction, block in ((0, behind), (1, ahead)):
                    along_z(direction, s, block, half, HALF).wait_recv()
                    if s < 3:
                        along_z(direction, s + 1, block, half, HALF).start()
                    else:
                        rows = pl.multiple_of(half + 32 * direction, 32)
                        along_z(direction, 4, block, rows, 32).start()
                    to_sibling(b + direction, block).start()

        @pl.when(b == 7)
        def _():
            block = (z + 4) % NZ
            for direction in (0, 1):
                rows = pl.multiple_of(half + 32 * direction, 32)
                along_z(direction, 4, block, rows, 32).wait_recv()
            to_sibling(7, block).start()

        @pl.when(b < NZ)
        def _():
            block = block_at(b)
            to_sibling(b, block).wait_recv()
            for lo, n in CHUNKS:
                prod[b, :, lo:lo + n] = jnp.dot(
                    st[block], weights[:, lo:lo + n], preferred_element_type=jnp.float32
                )
            for h in (0, 1):
                for lo, n in CHUNKS:
                    s1out[b, h, :, lo:lo + n] = coded(prod[b, rows_for(h, across), lo:lo + n])
                first_hop(b, h).start()

        @pl.when(jnp.logical_and(b >= 1, b < NZ + 1))
        def _():
            p = b - 1
            for h in (0, 1):
                to = right if h == 0 else left
                for lo, n in CHUNKS:
                    s2out[p, h, 16 * (1 - h):16 * (1 - h) + 16, lo:lo + n] = coded(
                        prod[p, rows_for(1 - h, to), lo:lo + n]
                    )
            for h in (0, 1):
                to = right if h == 0 else left
                first_hop(p, h).wait_recv()
                for lo, n in CHUNKS:
                    s2out[p, h, 16 * h:16 * h + 16, lo:lo + n] = coded(
                        prod[p, rows_for(h, to), lo:lo + n] + decoded(s1in[p, h, :, lo:lo + n])
                    )
                second_hop(p, h).start()

        @pl.when(b >= 2)
        def _():
            p = b - 2
            block = block_at(p)
            second_hop(p, 0).wait_recv()
            second_hop(p, 1).wait_recv()
            for h in (0, 1):
                top = jnp.full((PIECE, 1), -jnp.inf, jnp.float32)
                for lo, n in CHUNKS:
                    logits = prod[p, rows_for(h, x), lo:lo + n] + (
                        decoded(s2in[p, 0, 16 * h:16 * h + 16, lo:lo + n])
                        + decoded(s2in[p, 1, 16 * h:16 * h + 16, lo:lo + n])
                    )
                    acc[block, 16 * h:16 * h + 16, lo:lo + n] = logits
                    top = jnp.maximum(top, jnp.max(logits, axis=1, keepdims=True))
                col[block, 16 * h:16 * h + 16, :] = jnp.broadcast_to(top, (PIECE, 128))

        return carry

    lax.fori_loop(0, NZ + 2, step, 0)

    def exchanged(combine, base):
        row = jnp.transpose(col[...].reshape(256, 128))[0:1, :]
        ex1[base + q] = row
        first = [
            remote(
                ex1.at[base + q], ex1.at[base + q], e1s_sem.at[base + k], e1r_sem.at[base + k],
                in_plane((q + k) % (NY * NC)),
            )
            for k in range(1, NY * NC)
        ]
        for copy in first:
            copy.start()
        for copy in first:
            copy.wait_recv()
        row = ex1[base]
        for k in range(1, NY * NC):
            row = combine(row, ex1[base + k])
        ex2[base + z] = row
        second = [
            remote(
                ex2.at[base + z], ex2.at[base + z], e2s_sem.at[base + k], e2r_sem.at[base + k],
                at("z", (z + k) % NZ),
            )
            for k in range(1, NZ)
        ]
        for copy in second:
            copy.start()
        for copy in second:
            copy.wait_recv()
        row = ex2[base]
        for k in range(1, NZ):
            row = combine(row, ex2[base + k])
        return jnp.transpose(jnp.broadcast_to(row, (128, 256))), first + second

    top, sent_top = exchanged(jnp.maximum, 0)
    col[...] = top.reshape(NZ, 32, 128)

    def filter_rows(block, carry):
        for h in (0, 1):
            t = col[block, 16 * h:16 * h + 16, 0:1]
            total = jnp.zeros((PIECE, 1), jnp.float32)
            for lo, n in CHUNKS:
                shifted = acc[block, 16 * h:16 * h + 16, lo:lo + n] - t
                u = sharpness * (shifted + minp_offset)
                gated = shifted + (jnp.minimum(u, 0.0) - jnp.log1p(jnp.exp(-jnp.abs(u))))
                acc[block, 16 * h:16 * h + 16, lo:lo + n] = gated
                total = total + jnp.sum(jnp.exp(gated), axis=1, keepdims=True)
            col[block, 16 * h:16 * h + 16, :] = jnp.broadcast_to(total, (PIECE, 128))
        pltpu.make_async_copy(acc.at[block], gated_out.at[block], o_sem.at[block]).start()
        return carry

    lax.fori_loop(0, NZ, filter_rows, 0)
    total, sent_total = exchanged(jnp.add, 8)
    lnt_out[...] = jnp.log(total)

    for copy in x_copies + y_copies + sent_top + sent_total:
        copy.wait_send()
    for direction in (0, 1):
        for s in (1, 2, 3):
            along_z(direction, s, z, half, HALF).wait_send()
        along_z(direction, 4, z, half, 32).wait_send()

    def settle(b, carry):
        to_sibling(b, z).wait_send()
        for h in (0, 1):
            first_hop(b, h).wait_send()
            second_hop(b, h).wait_send()
        pltpu.make_async_copy(acc.at[b], gated_out.at[b], o_sem.at[b]).wait()
        return carry

    lax.fori_loop(0, NZ, settle, 0)


def body(states, head):
    dma = pltpu.SemaphoreType.DMA
    f32, bf16 = jnp.float32, jnp.bfloat16
    gated, lnt = pl.pallas_call(
        kernel,
        out_shape=(
            jax.ShapeDtypeStruct((NZ, 32, COLS), f32),
            jax.ShapeDtypeStruct((256, 128), f32),
        ),
        in_specs=[pl.BlockSpec(memory_space=pl.ANY)] * 2,
        out_specs=(
            pl.BlockSpec(memory_space=pl.ANY),
            pl.BlockSpec(memory_space=pltpu.VMEM),
        ),
        scratch_shapes=[
            pltpu.VMEM((DEPTH, COLS), bf16),
            pltpu.VMEM((NX, LOCAL, DEPTH), bf16),
            pltpu.VMEM((NZ, BLOCK, DEPTH), bf16),
            pltpu.VMEM((NZ, BLOCK, COLS), f32),
            pltpu.VMEM((NZ, 2, PIECE, COLS), bf16),
            pltpu.VMEM((NZ, 2, PIECE, COLS), bf16),
            pltpu.VMEM((NZ, 2, 2 * PIECE, COLS), bf16),
            pltpu.VMEM((NZ, 2, 2 * PIECE, COLS), bf16),
            pltpu.VMEM((NZ, 32, COLS), f32),
            pltpu.VMEM((NZ, 32, 128), f32),
            pltpu.VMEM((16, 1, 256), f32),
            pltpu.VMEM((16, 1, 256), f32),
            dma((7,)),
            dma,
            dma((3,)), dma((3,)),
            dma((3,)), dma((3,)),
            dma((2, 5)), dma((2, 5)),
            dma((8,)), dma((8,)),
            dma((8, 2)), dma((8, 2)),
            dma((8, 2)), dma((8, 2)),
            dma((16,)), dma((16,)),
            dma((16,)), dma((16,)),
            dma((8,)),
        ],
        compiler_params=pltpu.CompilerParams(
            collective_id=0, has_side_effects=True, vmem_limit_bytes=60 * 1024 * 1024
        ),
        name="minp",
    )(states, head)
    return jnp.maximum(gated.reshape(256, COLS) - lnt[:, :1], -logp_floor)


def solution(mesh):
    torus = Mesh(
        mesh.devices.reshape(NY, NZ, NC, NX),
        ("y", "z", "c", "x"),
    )
    return jax.shard_map(
        body,
        mesh=torus,
        in_specs=(P(VOCAB_HIDDEN, None), P("x", VOCAB)),
        out_specs=P("x", VOCAB),
        check_vma=False,
    )
```

time: 236 us -> 99.7 us (0.42)
  waiting for transfers between devices: 148 us -> 0 us
  Pallas kernels: 0 us -> 85.3 us
  blocking collectives: 53.7 us -> 0 us
  between operations: 13.1 us -> 0.04 us
  matrix products: 10.3 us -> 0 us
  local copies, waits for them, and re-layouts: 4.26 us -> 12.6 us
  other arithmetic: 6.69 us -> 1.46 us
    pallas_call x0 -> x1, Pallas kernels: none -> 85.3 us  [body(): pl.pallas_call(kernel, out_shape=(jax.ShapeDtypeStruct((NZ, 32, COLS), f3...]
    reduce_scatter x1 -> x0, waiting for transfers between devices: 83.2 us -> none  [body(): lax.psum_scatter(jnp.dot(gathered, head, preferred_element_type=jnp.float...]
    all_gather x2 -> x0, waiting for transfers between devices: 64.7 us -> none  [gather_in_order(): pieces = lax.all_gather(pieces, axes[k])]
    all_to_all x3 -> x0, blocking collectives: 43.1 us -> none  [the longest x2 33.9 us: from_everyone(): lax.all_to_all(jnp.broadcast_to(shard[None], (devices, *shard.shape)), ax...]
    all_gather x1 -> x0, blocking collectives: 10.6 us -> none  [gather_in_order(): pieces = lax.all_gather(pieces, axes[k])]
    dot_general x1 -> x0, matrix products: 10.3 us -> none  [body(): jnp.dot(gathered, head, preferred_element_type=jnp.float32)]
    unnamed x4 -> x3, local copies, waits for them, and re-layouts: 1.56 us -> 10.5 us
    transpose x1 -> x0, local copies, waits for them, and re-layouts: 2.6 us -> none  [gather_in_order(): pieces = pieces.transpose(*back, *range(len(axes), pieces.ndim))]
  transfers between devices with their start and end apart: 3 -> 0, of which waited for: 3 -> 0; matrix products, arithmetic and copies ran while one was open for 0% -> 0% of each run, Pallas kernels for 0% -> 0%
where the time goes in v1:
time: 99.7 us; the launch traced here: 99.3 us
  Pallas kernels  85.3 us (86%)
  local copies, waits for them, and re-layouts  12.6 us (13%)
  other arithmetic  1.46 us (1%)
    pallas_call x1, Pallas kernels, body(): pl.pallas_call(kernel, out_shape=(jax.ShapeDtypeStruct((NZ, 32, COLS), f3...  85.3 us
    unnamed x3, local copies, waits for them, and re-layouts  10.5 us

profile of v1, /device:TPU:1, one launch (start us, length us, event | category | flops | bytes accessed | tf_op | source)
XLA Modules:
  0.0 99.3 jit_solution(14120280817308000978)
XLA Ops:
  0.0 10.5 %copy.5.head = bf16[1792,2020]{1,0:T(8,128)(2,1)} copy(bf16[1792,2020]{0,1:T(8,128)(2,1)} %param.3) | data formatting | bytes 14479360 | tf_op args[1]
  10.5 85.3 %minp.1 = (f32[8,32,2020]{2,1,0:T(8,128)}, f32[256,128]{1,0:T(8,128)}) custom-call(bf16[4,7168]{1,0:T(4,128)(2,1)} %states.1, bf16[1792,2020]{1,0:T(8,128)(2,1)} %copy.5.head), custom_call_target="tpu_custom_call" | custom-call | tf_op jit(solution)/shard_map/minp/pallas_call | solution.py:302
  95.8 0.0 copy-start
  95.8 1.9 %copy.6 = f32[256,2020]{0,1:T(8,128)S(1)} copy(f32[256,2020]{1,0:T(8,128)} %bitcast.1) | data formatting | bytes 4136960 | tf_op jit(solution)/shard_map/reshape | solution.py:343
  97.8 0.0 copy-done
  97.8 0.1 slice_reduce_fusion
  97.9 1.5 %subtract_maximum_fusion = f32[256,2020]{0,1:T(8,128)} fusion(f32[256,2020]{0,1:T(8,128)S(1)} %copy.6, f32[256]{0:T(256)S(1)} %slice_reduce_fusion), kind=kLoop, calls=%fused_computation | loop fusion | flops 1034240 | bytes 4137984 | tf_op jit(solution)/shard_map/max | solution.py:343
Async XLA Ops:
  95.8 2.0 %copy-start = (f32[256,128]{1,0:T(8,128)S(1)}, f32[256,128]{1,0:T(8,128)}, u32[]{:S(2)}) copy-start(f32[256,128]{1,0:T(8,128)} %get-tuple-element.8) | copy-start | bytes 393220

commit v2 on v0

v2 whole, which is shorter than its diff:
```python
import math

import jax
import jax.numpy as jnp
from jax import lax
from jax.experimental import pallas as pl
from jax.experimental.pallas import tpu as pltpu
from jax.sharding import Mesh
from jax.sharding import PartitionSpec as P

MESH = pl.DeviceIdType.MESH
VOCAB = ("y", "z", "c")
VOCAB_HIDDEN = ("y", "z", "c", "x")
NX, NY, NZ, NC = 4, 4, 8, 2

sharpness = 4.0
minp_offset = math.log(10.0)
logp_floor = 30.0

BLOCK = 128
HALF = 64
PIECE = 16
LOCAL = 4
OWNED = 256
DEPTH = 1792
COLS = 2020
CHUNKS = ((0, 512), (512, 512), (1024, 512), (1536, 484))
POWER = 7
STEP = 224
TAIL = 9 * STEP

PLANE = [(dy, dx) for dy in range(NY) for dx in range(NX) if dy or dx]
PLANE.sort(key=lambda p: -(min(p[0], NY - p[0]) + min(p[1], NX - p[1])))
FAR = [(dy, dz) for dy in range(NY) for dz in range(NZ) if dy or dz]
FAR.sort(key=lambda p: -(min(p[0], NY - p[0]) + min(p[1], NZ - p[1])))


def coded(v):
    v2 = v * v
    v3 = v2 * v
    return (v3 * (v2 * v2)).astype(jnp.bfloat16)


def decoded(w):
    w = w.astype(jnp.float32)
    r = jnp.exp2(jnp.log2(jnp.abs(w)) * (1.0 / POWER))
    return jnp.where(w < 0.0, -r, r)


def lane_max(v):
    n = v.shape[1]
    best = v[:, 0:128]
    for lo in range(128, n, 128):
        part = v[:, lo:min(lo + 128, n)]
        if part.shape[1] < 128:
            fill = jnp.full((v.shape[0], 128 - part.shape[1]), -jnp.inf, v.dtype)
            part = jnp.concatenate([part, fill], axis=1)
        best = jnp.maximum(best, part)
    return best


def kernel(
    states, head, gated_out, lnt_out,
    raw, weights, xin, st, prod, s1out, s1in, s2out, s2in, acc, logits_t, gated, col, exc, exn,
    w_sem, xl_sem, xs_sem, xr_sem, zs_sem, zr_sem, cs_sem, cr_sem,
    s1s_sem, s1r_sem, s2s_sem, s2r_sem, ecs_sem, ecr_sem, ens_sem, enr_sem, o_sem,
):
    x, y, z, c = (lax.axis_index(n) for n in ("x", "y", "z", "c"))

    def at(dy=0, dz=0, dx=0, dc=0):
        return (
            (y + dy) % NY if dy else y,
            (z + dz) % NZ if dz else z,
            1 - c if dc else c,
            (x + dx) % NX if dx else x,
        )

    def remote(src, dst, send, recv, device):
        return pltpu.make_async_remote_copy(
            src_ref=src, dst_ref=dst, send_sem=send, recv_sem=recv,
            device_id=device, device_id_type=MESH,
        )

    w_copy = pltpu.make_async_copy(head, raw, w_sem)
    w_copy.start()
    own_piece = pltpu.make_async_copy(
        states.at[:, pl.ds(pl.multiple_of(x * DEPTH, 128), DEPTH)], xin.at[y * NX + x], xl_sem
    )
    own_piece.start()

    barrier = pltpu.get_barrier_semaphore()
    partners = [at(dy=dy, dx=dx) for dy, dx in PLANE]
    partners += [at(dz=1), at(dz=NZ - 1), at(dc=1)]
    for device in partners:
        pl.semaphore_signal(barrier, inc=1, device_id=device, device_id_type=MESH)
    pl.semaphore_wait(barrier, len(partners))

    x_copies = []
    for k, (dy, dx) in enumerate(PLANE):
        to = (x + dx) % NX
        x_copies.append(remote(
            states.at[:, pl.ds(pl.multiple_of(to * DEPTH, 128), DEPTH)], xin.at[y * NX + x],
            xs_sem.at[k], xr_sem.at[k], at(dy=dy, dx=dx),
        ))
        x_copies[-1].start()

    w_copy.wait()
    for lo in range(0, COLS, 256):
        n = min(256, COLS - lo)
        weights[:, lo:lo + n] = jnp.transpose(raw[lo:lo + n, :])

    own_piece.wait()
    for copy in x_copies:
        copy.wait_recv()
    half = pl.multiple_of(c * HALF, HALF)
    for j in range(NY):
        pieces = [xin[j * NX + k].astype(jnp.float32) for k in range(NX)]
        st[0, pl.ds(pl.multiple_of(half + j * PIECE, PIECE), PIECE), :] = jnp.concatenate(
            pieces, axis=0
        ).astype(jnp.bfloat16)

    def along_z(direction, s):
        source = 0 if s == 1 else 2 * s - 3 + direction
        target = 2 * s - 1 + direction if s < 4 else 7
        if s < 4:
            rows = pl.ds(half, HALF)
        else:
            rows = pl.ds(pl.multiple_of(half + 32 * direction, 32), 32)
        return remote(
            st.at[source, rows, :], st.at[target, rows, :],
            zs_sem.at[direction, s], zr_sem.at[direction, s],
            at(dz=1 if direction == 0 else NZ - 1),
        )

    def to_sibling(b):
        there = st.at[b, pl.ds(half, HALF), :]
        return remote(there, there, cs_sem.at[b], cr_sem.at[b], at(dc=1))

    to_sibling(0).start()
    along_z(0, 1).start()
    along_z(1, 1).start()

    right, left, across = (x + 1) % NX, (x + NX - 1) % NX, (x + 2) % NX

    def first_hop(b, h):
        return remote(
            s1out.at[b, h], s1in.at[b, h], s1s_sem.at[b, h], s1r_sem.at[b, h],
            at(dx=1 if h == 0 else NX - 1),
        )

    def second_hop(b, h):
        return remote(
            s2out.at[b, h], s2in.at[b, h], s2s_sem.at[b, h], s2r_sem.at[b, h],
            at(dx=1 if h == 0 else NX - 1),
        )

    def rows_for(h, d):
        return pl.ds(pl.multiple_of(h * HALF + d * PIECE, PIECE), PIECE)

    def multiply(b, carry):
        to_sibling(b).wait_recv()
        for lo, n in CHUNKS:
            prod[b, :, lo:lo + n] = jnp.dot(
                st[b], weights[:, lo:lo + n], preferred_element_type=jnp.float32
            )
        for h in (0, 1):
            for lo, n in CHUNKS:
                s1out[b, h, :, lo:lo + n] = coded(prod[b, rows_for(h, across), lo:lo + n])
            first_hop(b, h).start()
        return carry

    def relay(b, carry):
        for h in (0, 1):
            to = right if h == 0 else left
            for lo, n in CHUNKS:
                s2out[b, h, 16 * (1 - h):16 * (1 - h) + 16, lo:lo + n] = coded(
                    prod[b, rows_for(1 - h, to), lo:lo + n]
                )
        for h in (0, 1):
            to = right if h == 0 else left
            first_hop(b, h).wait_recv()
            for lo, n in CHUNKS:
                s2out[b, h, 16 * h:16 * h + 16, lo:lo + n] = coded(
                    prod[b, rows_for(h, to), lo:lo + n] + decoded(s1in[b, h, :, lo:lo + n])
                )
            second_hop(b, h).start()
        return carry

    def collect(b, carry):
        s = (b + 1) // 2
        block = (z + s * (1 - 2 * (b % 2)) + NZ) % NZ
        second_hop(b, 0).wait_recv()
        second_hop(b, 1).wait_recv()
        for h in (0, 1):
            rows = slice(16 * h, 16 * h + 16)
            best = None
            for lo, n in CHUNKS:
                logits = prod[b, rows_for(h, x), lo:lo + n] + (
                    decoded(s2in[b, 0, rows, lo:lo + n]) + decoded(s2in[b, 1, rows, lo:lo + n])
                )
                acc[block, rows, lo:lo + n] = logits
                part = lane_max(logits)
                best = part if best is None else jnp.maximum(best, part)
            col[block, rows, :] = best
        return carry

    def pair(i, carry):
        for s in (1, 2, 3, 4):
            @pl.when(i == s)
            def _():
                for direction in (0, 1):
                    along_z(direction, s).wait_recv()
                    if s < 4:
                        along_z(direction, s + 1).start()
                        to_sibling(2 * s - 1 + direction).start()
                if s == 4:
                    to_sibling(7).start()

        lo, hi = jnp.maximum(2 * i - 1, 0), jnp.minimum(2 * i + 1, NZ)
        lax.fori_loop(lo, hi, multiply, 0)
        lax.fori_loop(lo, hi, relay, 0)
        lax.fori_loop(jnp.maximum(2 * i - 3, 0), jnp.minimum(lo, NZ), collect, 0)
        return carry

    lax.fori_loop(0, NZ // 2 + 2, pair, 0)

    def exchanged(phase, row, combine, meanwhile):
        exc[phase, 0] = row
        sibling = remote(
            exc.at[phase, 0], exc.at[phase, 1], ecs_sem.at[phase], ecr_sem.at[phase], at(dc=1)
        )
        sibling.start()
        sibling.wait_recv()
        exn[phase, 0] = combine(row, exc[phase, 1])
        copies = []
        for k, (dy, dz) in enumerate(FAR):
            copies.append(remote(
                exn.at[phase, 0], exn.at[phase, k + 1], ens_sem.at[phase, k], enr_sem.at[phase],
                at(dy=dy, dz=dz),
            ))
            copies[-1].start()
        meanwhile()
        arrived = exn.at[phase, pl.ds(1, len(FAR))]
        remote(arrived, arrived, ens_sem.at[phase, 0], enr_sem.at[phase], at(dz=1)).wait_recv()
        row = exn[phase, 0]
        for k in range(len(FAR)):
            row = combine(row, exn[phase, k + 1])
        return row, [sibling] + copies

    def transposed():
        for g in (0, 1):
            for lo in range(0, COLS, 128):
                n = min(128, COLS - lo)
                tile = acc[4 * g:4 * g + 4, :, lo:lo + n].reshape(128, n)
                logits_t[lo:lo + n, 128 * g:128 * g + 128] = jnp.transpose(tile)

    best = jnp.max(jnp.transpose(col[...].reshape(OWNED, 128)), axis=0, keepdims=True)
    top, sent = exchanged(0, best, jnp.maximum, transposed)

    cut = math.exp(-sharpness * minp_offset)

    def kept(v):
        a = jnp.exp(v - top)
        a4 = (a * a) * (a * a)
        return (a4 * a) / (a4 + cut)

    def add_rows(k, total):
        mass = kept(logits_t[pl.ds(pl.multiple_of(k * STEP, 8), STEP), :])
        return total + jnp.sum(mass.reshape(STEP // 8, 8, OWNED), axis=0)

    total = lax.fori_loop(0, TAIL // STEP, add_rows, jnp.zeros((8, OWNED), jnp.float32))
    total = jnp.sum(total, axis=0, keepdims=True) + jnp.sum(
        kept(logits_t[TAIL:COLS, :]), axis=0, keepdims=True
    )

    def filtered(v):
        shifted = v - top
        u = sharpness * (shifted + minp_offset)
        return shifted + (jnp.minimum(u, 0.0) - jnp.log1p(jnp.exp(-jnp.abs(u))))

    def filter_all():
        def rows(k, carry):
            here = pl.ds(pl.multiple_of(k * STEP, 8), STEP)
            gated[here, :] = filtered(logits_t[here, :])
            return carry

        lax.fori_loop(0, TAIL // STEP, rows, 0)
        gated[TAIL:COLS, :] = filtered(logits_t[TAIL:COLS, :])
        pltpu.make_async_copy(gated, gated_out, o_sem).start()

    total, more = exchanged(1, total, jnp.add, filter_all)
    lnt_out[...] = jnp.log(total)

    for copy in x_copies + sent + more:
        copy.wait_send()
    for direction in (0, 1):
        for s in (1, 2, 3, 4):
            along_z(direction, s).wait_send()

    def settle(b, carry):
        to_sibling(b).wait_send()
        for h in (0, 1):
            first_hop(b, h).wait_send()
            second_hop(b, h).wait_send()
        return carry

    lax.fori_loop(0, NZ, settle, 0)
    pltpu.make_async_copy(gated, gated_out, o_sem).wait()


def body(states, head):
    dma = pltpu.SemaphoreType.DMA
    f32, bf16 = jnp.float32, jnp.bfloat16
    gated, lnt = pl.pallas_call(
        kernel,
        out_shape=(
            jax.ShapeDtypeStruct((COLS, OWNED), f32),
            jax.ShapeDtypeStruct((1, OWNED), f32),
        ),
        in_specs=[pl.BlockSpec(memory_space=pl.ANY)] * 2,
        out_specs=(
            pl.BlockSpec(memory_space=pl.ANY),
            pl.BlockSpec(memory_space=pltpu.VMEM),
        ),
        scratch_shapes=[
            pltpu.VMEM((COLS, DEPTH), bf16),
            pltpu.VMEM((DEPTH, COLS), bf16),
            pltpu.VMEM((NY * NX, LOCAL, DEPTH), bf16),
            pltpu.VMEM((NZ, BLOCK, DEPTH), bf16),
            pltpu.VMEM((NZ, BLOCK, COLS), f32),
            pltpu.VMEM((NZ, 2, PIECE, COLS), bf16),
            pltpu.VMEM((NZ, 2, PIECE, COLS), bf16),
            pltpu.VMEM((NZ, 2, 2 * PIECE, COLS), bf16),
            pltpu.VMEM((NZ, 2, 2 * PIECE, COLS), bf16),
            pltpu.VMEM((NZ, 32, COLS), f32),
            pltpu.VMEM((COLS, OWNED), f32),
            pltpu.VMEM((COLS, OWNED), f32),
            pltpu.VMEM((NZ, 32, 128), f32),
            pltpu.VMEM((2, 2, 1, OWNED), f32),
            pltpu.VMEM((2, len(FAR) + 1, 1, OWNED), f32),
            dma,
            dma,
            dma((len(PLANE),)), dma((len(PLANE),)),
            dma((2, 5)), dma((2, 5)),
            dma((NZ,)), dma((NZ,)),
            dma((NZ, 2)), dma((NZ, 2)),
            dma((NZ, 2)), dma((NZ, 2)),
            dma((2,)), dma((2,)),
            dma((2, len(FAR))), dma((2,)),
            dma,
        ],
        compiler_params=pltpu.CompilerParams(
            collective_id=0, has_side_effects=True, vmem_limit_bytes=56 * 1024 * 1024
        ),
        name="minp",
    )(states, head.T)
    return jnp.maximum(gated - lnt, -logp_floor).T


def solution(mesh):
    torus = Mesh(
        mesh.devices.reshape(NY, NZ, NC, NX),
        ("y", "z", "c", "x"),
    )
    return jax.shard_map(
        body,
        mesh=torus,
        in_specs=(P(VOCAB_HIDDEN, None), P("x", VOCAB)),
        out_specs=P("x", VOCAB),
        check_vma=False,
    )
```

time: 236 us -> 80 us (0.34)
  waiting for transfers between devices: 148 us -> 0 us
  Pallas kernels: 0 us -> 76.9 us
  blocking collectives: 53.7 us -> 0 us
  between operations: 13.1 us -> 0.01 us
  matrix products: 10.3 us -> 0 us
  local copies, waits for them, and re-layouts: 4.26 us -> 0 us
  other arithmetic: 6.69 us -> 3.03 us
    reduce_scatter x1 -> x0, waiting for transfers between devices: 83.2 us -> none  [body(): lax.psum_scatter(jnp.dot(gathered, head, preferred_element_type=jnp.float...]
    pallas_call x0 -> x1, Pallas kernels: none -> 76.9 us  [body(): pl.pallas_call(kernel, out_shape=(jax.ShapeDtypeStruct((COLS, OWNED), f32...]
    all_gather x2 -> x0, waiting for transfers between devices: 64.7 us -> none  [gather_in_order(): pieces = lax.all_gather(pieces, axes[k])]
    all_to_all x3 -> x0, blocking collectives: 43.1 us -> none  [the longest x2 33.9 us: from_everyone(): lax.all_to_all(jnp.broadcast_to(shard[None], (devices, *shard.shape)), ax...]
    all_gather x1 -> x0, blocking collectives: 10.6 us -> none  [gather_in_order(): pieces = lax.all_gather(pieces, axes[k])]
    dot_general x1 -> x0, matrix products: 10.3 us -> none  [body(): jnp.dot(gathered, head, preferred_element_type=jnp.float32)]
    transpose x0 -> x1, other arithmetic: none -> 3.03 us  [body(): return jnp.maximum(gated - lnt, -logp_floor).T]
    max x1 -> x0, other arithmetic: 2.86 us -> none  [body(): return jnp.maximum(gated - jnp.log(total)[:, None], -logp_floor)]
  transfers between devices with their start and end apart: 3 -> 0, of which waited for: 3 -> 0; matrix products, arithmetic and copies ran while one was open for 0% -> 0% of each run, Pallas kernels for 0% -> 0%
where the time goes in v2:
time: 80 us; the launch traced here: 79.9 us
  Pallas kernels  76.9 us (96%)
  other arithmetic  3.03 us (4%)
    pallas_call x1, Pallas kernels, body(): pl.pallas_call(kernel, out_shape=(jax.ShapeDtypeStruct((COLS, OWNED), f32...  76.9 us
    transpose x1, other arithmetic, body(): return jnp.maximum(gated - lnt, -logp_floor).T  3.03 us

profile of v2, /device:TPU:1, one launch (start us, length us, event | category | flops | bytes accessed | tf_op | source)
XLA Modules:
  0.0 79.9 jit_solution(6501057700137465784)
XLA Ops:
  0.0 76.9 %minp.1 = (f32[2020,256]{1,0:T(8,128)}, f32[1,256]{1,0:T(1,128)}) custom-call(bf16[4,7168]{1,0:T(4,128)(2,1)} %states.1, bf16[2020,1792]{1,0:T(8,128)(2,1)} %bitcast.4), custom_call_target="tpu_custom_call" | custom-call | tf_op jit(solution)/shard_map/minp/pallas_call | solution.py:314
  76.9 3.0 %maximum_bitcast_fusion = f32[256,2020]{0,1:T(8,128)} fusion(f32[2020,256]{1,0:T(8,128)} %get-tuple-element.7, f32[256]{0:T(256)} %bitcast.5), kind=kLoop, calls=%fused_computation | loop fusion | flops 1034240 | bytes 4137984 | tf_op jit(solution)/shard_map/transpose | solution.py:357

commit v3 on v2

--- a/solution.py
+++ b/solution.py
@@ -19,6 +19,7 @@
 
 BLOCK = 128
 HALF = 64
+SHARE = 32
 PIECE = 16
 LOCAL = 4
 OWNED = 256
@@ -29,7 +30,7 @@
 STEP = 224
 TAIL = 9 * STEP
 
-PLANE = [(dy, dx) for dy in range(NY) for dx in range(NX) if dy or dx]
+PLANE = [(dy, dx) for dy in range(NY) for dx in range(NX)]
 PLANE.sort(key=lambda p: -(min(p[0], NY - p[0]) + min(p[1], NX - p[1])))
 FAR = [(dy, dz) for dy in range(NY) for dz in range(NZ) if dy or dz]
 FAR.sort(key=lambda p: -(min(p[0], NY - p[0]) + min(p[1], NZ - p[1])))
@@ -83,62 +84,79 @@
 
     w_copy = pltpu.make_async_copy(head, raw, w_sem)
     w_copy.start()
+    keeper = y // 2
+    slot = (y % 2) * 8 + c * NX + x
+    stays = keeper == c
+
+    barrier = pltpu.get_barrier_semaphore()
+
+    def greet(device):
+        pl.semaphore_signal(barrier, inc=1, device_id=device, device_id_type=MESH)
+
+    for dx in range(NX):
+        for j in range(2):
+            for cc in range(NC):
+                sender = (2 * c + j, z, cc, (x + dx) % NX)
+                if dx:
+                    greet(sender)
+                else:
+                    @pl.when(jnp.logical_or(2 * c + j != y, cc != c))
+                    def _():
+                        greet(sender)
+    for device in (at(dz=1), at(dz=NZ - 1), at(dc=1)):
+        greet(device)
+    pl.semaphore_wait(barrier, 19 - stays.astype(jnp.int32))
+
+    def piece(k, dy, dx):
+        to = (x + dx) % NX
+        return remote(
+            states.at[:, pl.ds(pl.multiple_of(to * DEPTH, 128), DEPTH)], xin.at[slot],
+            xs_sem.at[k], xr_sem.at[slot], ((y + dy) % NY, z, keeper, to),
+        )
+
     own_piece = pltpu.make_async_copy(
-        states.at[:, pl.ds(pl.multiple_of(x * DEPTH, 128), DEPTH)], xin.at[y * NX + x], xl_sem
+        states.at[:, pl.ds(pl.multiple_of(x * DEPTH, 128), DEPTH)], xin.at[slot], xl_sem
     )
-    own_piece.start()
-
-    barrier = pltpu.get_barrier_semaphore()
-    partners = [at(dy=dy, dx=dx) for dy, dx in PLANE]
-    partners += [at(dz=1), at(dz=NZ - 1), at(dc=1)]
-    for device in partners:
-        pl.semaphore_signal(barrier, inc=1, device_id=device, device_id_type=MESH)
-    pl.semaphore_wait(barrier, len(partners))
-
-    x_copies = []
     for k, (dy, dx) in enumerate(PLANE):
-        to = (x + dx) % NX
-        x_copies.append(remote(
-            states.at[:, pl.ds(pl.multiple_of(to * DEPTH, 128), DEPTH)], xin.at[y * NX + x],
-            xs_sem.at[k], xr_sem.at[k], at(dy=dy, dx=dx),
-        ))
-        x_copies[-1].start()
+        if dy or dx:
+            piece(k, dy, dx).start()
+        else:
+            pl.when(jnp.logical_not(stays))(lambda: piece(k, 0, 0).start())
+            pl.when(stays)(own_piece.start)
 
     w_copy.wait()
     for lo in range(0, COLS, 256):
         n = min(256, COLS - lo)
         weights[:, lo:lo + n] = jnp.transpose(raw[lo:lo + n, :])
 
-    own_piece.wait()
-    for copy in x_copies:
-        copy.wait_recv()
-    half = pl.multiple_of(c * HALF, HALF)
-    for j in range(NY):
-        pieces = [xin[j * NX + k].astype(jnp.float32) for k in range(NX)]
-        st[0, pl.ds(pl.multiple_of(half + j * PIECE, PIECE), PIECE), :] = jnp.concatenate(
-            pieces, axis=0
-        ).astype(jnp.bfloat16)
-
-    def along_z(direction, s):
-        source = 0 if s == 1 else 2 * s - 3 + direction
-        target = 2 * s - 1 + direction if s < 4 else 7
-        if s < 4:
-            rows = pl.ds(half, HALF)
-        else:
-            rows = pl.ds(pl.multiple_of(half + 32 * direction, 32), 32)
+    pl.when(stays)(own_piece.wait)
+    for k in range(4 * NX):
+        arrived = remote(xin.at[k], xin.at[k], xs_sem.at[k], xr_sem.at[k], at(dc=1))
+        pl.when(jnp.logical_or(jnp.logical_not(stays), k != slot))(arrived.wait_recv)
+    for j in range(2):
+        for cc in range(NC):
+            pieces = [xin[j * 8 + cc * NX + k].astype(jnp.float32) for k in range(NX)]
+            rows = pl.ds(pl.multiple_of(cc * HALF + c * SHARE + j * PIECE, PIECE), PIECE)
+            st[0, rows, :] = jnp.concatenate(pieces, axis=0).astype(jnp.bfloat16)
+
+    def share(b, h):
+        return st.at[b, pl.ds(pl.multiple_of(h * HALF + c * SHARE, SHARE), SHARE), :]
+
+    def along_z(source, source_h, target, target_h, way):
         return remote(
-            st.at[source, rows, :], st.at[target, rows, :],
-            zs_sem.at[direction, s], zr_sem.at[direction, s],
-            at(dz=1 if direction == 0 else NZ - 1),
-        )
-
-    def to_sibling(b):
-        there = st.at[b, pl.ds(half, HALF), :]
-        return remote(there, there, cs_sem.at[b], cr_sem.at[b], at(dc=1))
-
-    to_sibling(0).start()
-    along_z(0, 1).start()
-    along_z(1, 1).start()
+            share(source, source_h), share(target, target_h),
+            zs_sem.at[target, target_h], zr_sem.at[target, target_h],
+            (y, (z + 1 - 2 * way + NZ) % NZ, c, x),
+        )
+
+    def to_sibling(b, h):
+        return remote(share(b, h), share(b, h), cs_sem.at[b, h], cr_sem.at[b, h], at(dc=1))
+
+    for h in (0, 1):
+        to_sibling(0, h).start()
+    for p in (0, 1):
+        for way in (0, 1):
+            along_z(0, p, 1 + p, way, way).start()
 
     right, left, across = (x + 1) % NX, (x + NX - 1) % NX, (x + 2) % NX
 
@@ -157,8 +175,9 @@
     def rows_for(h, d):
         return pl.ds(pl.multiple_of(h * HALF + d * PIECE, PIECE), PIECE)
 
-    def multiply(b, carry):
-        to_sibling(b).wait_recv()
+    def multiply(b):
+        for h in (0, 1):
+            to_sibling(b, h).wait_recv()
         for lo, n in CHUNKS:
             prod[b, :, lo:lo + n] = jnp.dot(
                 st[b], weights[:, lo:lo + n], preferred_element_type=jnp.float32
@@ -167,9 +186,8 @@
             for lo, n in CHUNKS:
                 s1out[b, h, :, lo:lo + n] = coded(prod[b, rows_for(h, across), lo:lo + n])
             first_hop(b, h).start()
-        return carry
-
-    def relay(b, carry):
+
+    def relay(b):
         for h in (0, 1):
             to = right if h == 0 else left
             for lo, n in CHUNKS:
@@ -184,45 +202,50 @@
                     prod[b, rows_for(h, to), lo:lo + n] + decoded(s1in[b, h, :, lo:lo + n])
                 )
             second_hop(b, h).start()
-        return carry
-
-    def collect(b, carry):
+
+    def collect(b):
+        alone = jnp.logical_or(b == 0, b == NZ - 1)
         s = (b + 1) // 2
-        block = (z + s * (1 - 2 * (b % 2)) + NZ) % NZ
         second_hop(b, 0).wait_recv()
         second_hop(b, 1).wait_recv()
         for h in (0, 1):
             rows = slice(16 * h, 16 * h + 16)
+            block = jnp.where(alone, z + s, z + NZ + (2 * h - 1) * s) % NZ
+            core = jnp.where(alone, h, 1 - b % 2)
+            mine = pl.ds(pl.multiple_of(core * PIECE, PIECE), PIECE)
             best = None
             for lo, n in CHUNKS:
                 logits = prod[b, rows_for(h, x), lo:lo + n] + (
                     decoded(s2in[b, 0, rows, lo:lo + n]) + decoded(s2in[b, 1, rows, lo:lo + n])
                 )
-                acc[block, rows, lo:lo + n] = logits
+                acc[block, mine, lo:lo + n] = logits
                 part = lane_max(logits)
                 best = part if best is None else jnp.maximum(best, part)
-            col[block, rows, :] = best
+            col[block, mine, :] = best
+
+    def pass_on(b):
+        for h in (0, 1):
+            along_z(b, h, b, h, h).wait_recv()
+
+            @pl.when(b <= 4)
+            def _():
+                along_z(b, h, b + 2, h, h).start()
+
+            to_sibling(b, h).start()
+
+        @pl.when(jnp.logical_or(b == 5, b == 6))
+        def _():
+            p = 1 - b % 2
+            along_z(b, p, 7, p, p).start()
+
+    def step(b, carry):
+        pl.when(b < NZ)(lambda: multiply(b))
+        pl.when(b < NZ - 1)(lambda: pass_on(b + 1))
+        pl.when(jnp.logical_and(b != 1, b <= NZ))(lambda: relay(jnp.maximum(b - 1, 0)))
+        pl.when(b >= 3)(lambda: collect(b - 3))
         return carry
 
-    def pair(i, carry):
-        for s in (1, 2, 3, 4):
-            @pl.when(i == s)
-            def _():
-                for direction in (0, 1):
-                    along_z(direction, s).wait_recv()
-                    if s < 4:
-                        along_z(direction, s + 1).start()
-                        to_sibling(2 * s - 1 + direction).start()
-                if s == 4:
-                    to_sibling(7).start()
-
-        lo, hi = jnp.maximum(2 * i - 1, 0), jnp.minimum(2 * i + 1, NZ)
-        lax.fori_loop(lo, hi, multiply, 0)
-        lax.fori_loop(lo, hi, relay, 0)
-        lax.fori_loop(jnp.maximum(2 * i - 3, 0), jnp.minimum(lo, NZ), collect, 0)
-        return carry
-
-    lax.fori_loop(0, NZ // 2 + 2, pair, 0)
+    lax.fori_loop(0, NZ + 3, step, 0)
 
     def exchanged(phase, row, combine, meanwhile):
         exc[phase, 0] = row
@@ -291,15 +314,18 @@
     total, more = exchanged(1, total, jnp.add, filter_all)
     lnt_out[...] = jnp.log(total)
 
-    for copy in x_copies + sent + more:
+    for k, (dy, dx) in enumerate(PLANE):
+        if dy or dx:
+            piece(k, dy, dx).wait_send()
+        else:
+            pl.when(jnp.logical_not(stays))(lambda: piece(k, 0, 0).wait_send())
+    for copy in sent + more:
         copy.wait_send()
-    for direction in (0, 1):
-        for s in (1, 2, 3, 4):
-            along_z(direction, s).wait_send()
 
     def settle(b, carry):
-        to_sibling(b).wait_send()
-        for h in (0, 1):
+        for h in (0, 1):
+            pl.when(b >= 1)(along_z(b, h, b, h, h).wait_send)
+            to_sibling(b, h).wait_send()
             first_hop(b, h).wait_send()
             second_hop(b, h).wait_send()
         return carry
@@ -341,8 +367,8 @@
             dma,
             dma,
             dma((len(PLANE),)), dma((len(PLANE),)),
-            dma((2, 5)), dma((2, 5)),
-            dma((NZ,)), dma((NZ,)),
+            dma((NZ, 2)), dma((NZ, 2)),
+            dma((NZ, 2)), dma((NZ, 2)),
             dma((NZ, 2)), dma((NZ, 2)),
             dma((NZ, 2)), dma((NZ, 2)),
             dma((2,)), dma((2,)),

time: 80 us -> 76.9 us (0.961)
  Pallas kernels: 76.9 us -> 73.8 us
    pallas_call x1, Pallas kernels: 76.9 us -> 73.8 us  [body(): pl.pallas_call(kernel, out_shape=(jax.ShapeDtypeStruct((COLS, OWNED), f32...]
where the time goes in v3:
time: 76.9 us; the launch traced here: 76.8 us
  Pallas kernels  73.8 us (96%)
  other arithmetic  3.03 us (4%)
    pallas_call x1, Pallas kernels, body(): pl.pallas_call(kernel, out_shape=(jax.ShapeDtypeStruct((COLS, OWNED), f32...  73.8 us
    transpose x1, other arithmetic, body(): return jnp.maximum(gated - lnt, -logp_floor).T  3.03 us

profile of v3, /device:TPU:1, one launch (start us, length us, event | category | flops | bytes accessed | tf_op | source)
XLA Modules:
  0.0 76.8 jit_solution(9592958470902846358)
XLA Ops:
  0.0 73.8 %minp.1 = (f32[2020,256]{1,0:T(8,128)}, f32[1,256]{1,0:T(1,128)}) custom-call(bf16[4,7168]{1,0:T(4,128)(2,1)} %states.1, bf16[2020,1792]{1,0:T(8,128)(2,1)} %bitcast.4), custom_call_target="tpu_custom_call" | custom-call | tf_op jit(solution)/shard_map/minp/pallas_call | solution.py:340
  73.8 3.0 %maximum_bitcast_fusion = f32[256,2020]{0,1:T(8,128)} fusion(f32[2020,256]{1,0:T(8,128)} %get-tuple-element.7, f32[256]{0:T(256)} %bitcast.5), kind=kLoop, calls=%fused_computation | loop fusion | flops 1034240 | bytes 4137984 | tf_op jit(solution)/shard_map/transpose | solution.py:383

commit v4 on v3

--- a/solution.py
+++ b/solution.py
@@ -61,10 +61,10 @@
 
 
 def kernel(
-    states, head, gated_out, lnt_out,
-    raw, weights, xin, st, prod, s1out, s1in, s2out, s2in, acc, logits_t, gated, col, exc, exn,
+    states, head, gated, lnt_out,
+    raw, weights, xin, st, prod, s1out, s1in, s2out, s2in, acc, logits_t, col, exc, exn,
     w_sem, xl_sem, xs_sem, xr_sem, zs_sem, zr_sem, cs_sem, cr_sem,
-    s1s_sem, s1r_sem, s2s_sem, s2r_sem, ecs_sem, ecr_sem, ens_sem, enr_sem, o_sem,
+    s1s_sem, s1r_sem, s2s_sem, s2r_sem, ecs_sem, ecr_sem, ens_sem, enr_sem,
 ):
     x, y, z, c = (lax.axis_index(n) for n in ("x", "y", "z", "c"))
 
@@ -255,22 +255,36 @@
         sibling.start()
         sibling.wait_recv()
         exn[phase, 0] = combine(row, exc[phase, 1])
-        copies = []
         for k, (dy, dz) in enumerate(FAR):
-            copies.append(remote(
-                exn.at[phase, 0], exn.at[phase, k + 1], ens_sem.at[phase, k], enr_sem.at[phase],
+            remote(
+                exn.at[phase, 0], exn.at[phase, k + 1], ens_sem.at[phase], enr_sem.at[phase],
                 at(dy=dy, dz=dz),
-            ))
-            copies[-1].start()
+            ).start()
         meanwhile()
         arrived = exn.at[phase, pl.ds(1, len(FAR))]
-        remote(arrived, arrived, ens_sem.at[phase, 0], enr_sem.at[phase], at(dz=1)).wait_recv()
+        everyone = remote(arrived, arrived, ens_sem.at[phase], enr_sem.at[phase], at(dz=1))
+        sibling.wait_send()
+        everyone.wait_recv()
         row = exn[phase, 0]
         for k in range(len(FAR)):
             row = combine(row, exn[phase, k + 1])
-        return row, [sibling] + copies
+        return row, everyone
+
+    def settle(b, carry):
+        for h in (0, 1):
+            pl.when(b >= 1)(along_z(b, h, b, h, h).wait_send)
+            to_sibling(b, h).wait_send()
+            first_hop(b, h).wait_send()
+            second_hop(b, h).wait_send()
+        return carry
 
     def transposed():
+        for k, (dy, dx) in enumerate(PLANE):
+            if dy or dx:
+                piece(k, dy, dx).wait_send()
+            else:
+                pl.when(jnp.logical_not(stays))(lambda: piece(k, 0, 0).wait_send())
+        lax.fori_loop(0, NZ, settle, 0)
         for g in (0, 1):
             for lo in range(0, COLS, 128):
                 n = min(128, COLS - lo)
@@ -278,7 +292,7 @@
                 logits_t[lo:lo + n, 128 * g:128 * g + 128] = jnp.transpose(tile)
 
     best = jnp.max(jnp.transpose(col[...].reshape(OWNED, 128)), axis=0, keepdims=True)
-    top, sent = exchanged(0, best, jnp.maximum, transposed)
+    top, sent_top = exchanged(0, best, jnp.maximum, transposed)
 
     cut = math.exp(-sharpness * minp_offset)
 
@@ -309,29 +323,12 @@
 
         lax.fori_loop(0, TAIL // STEP, rows, 0)
         gated[TAIL:COLS, :] = filtered(logits_t[TAIL:COLS, :])
-        pltpu.make_async_copy(gated, gated_out, o_sem).start()
-
-    total, more = exchanged(1, total, jnp.add, filter_all)
+
+    total, sent_total = exchanged(1, total, jnp.add, filter_all)
     lnt_out[...] = jnp.log(total)
 
-    for k, (dy, dx) in enumerate(PLANE):
-        if dy or dx:
-            piece(k, dy, dx).wait_send()
-        else:
-            pl.when(jnp.logical_not(stays))(lambda: piece(k, 0, 0).wait_send())
-    for copy in sent + more:
-        copy.wait_send()
-
-    def settle(b, carry):
-        for h in (0, 1):
-            pl.when(b >= 1)(along_z(b, h, b, h, h).wait_send)
-            to_sibling(b, h).wait_send()
-            first_hop(b, h).wait_send()
-            second_hop(b, h).wait_send()
-        return carry
-
-    lax.fori_loop(0, NZ, settle, 0)
-    pltpu.make_async_copy(gated, gated_out, o_sem).wait()
+    sent_top.wait_send()
+    sent_total.wait_send()
 
 
 def body(states, head):
@@ -343,11 +340,8 @@
             jax.ShapeDtypeStruct((COLS, OWNED), f32),
             jax.ShapeDtypeStruct((1, OWNED), f32),
         ),
-        in_specs=[pl.BlockSpec(memory_space=pl.ANY)] * 2,
-        out_specs=(
-            pl.BlockSpec(memory_space=pl.ANY),
-            pl.BlockSpec(memory_space=pltpu.VMEM),
-        ),
+        in_specs=[pl.BlockSpec(memory_space=pltpu.HBM)] * 2,
+        out_specs=(pl.BlockSpec(memory_space=pltpu.VMEM),) * 2,
         scratch_shapes=[
             pltpu.VMEM((COLS, DEPTH), bf16),
             pltpu.VMEM((DEPTH, COLS), bf16),
@@ -360,7 +354,6 @@
             pltpu.VMEM((NZ, 2, 2 * PIECE, COLS), bf16),
             pltpu.VMEM((NZ, 32, COLS), f32),
             pltpu.VMEM((COLS, OWNED), f32),
-            pltpu.VMEM((COLS, OWNED), f32),
             pltpu.VMEM((NZ, 32, 128), f32),
             pltpu.VMEM((2, 2, 1, OWNED), f32),
             pltpu.VMEM((2, len(FAR) + 1, 1, OWNED), f32),
@@ -372,14 +365,16 @@
             dma((NZ, 2)), dma((NZ, 2)),
             dma((NZ, 2)), dma((NZ, 2)),
             dma((2,)), dma((2,)),
-            dma((2, len(FAR))), dma((2,)),
-            dma,
+            dma((2,)), dma((2,)),
         ],
         compiler_params=pltpu.CompilerParams(
-            collective_id=0, has_side_effects=True, vmem_limit_bytes=56 * 1024 * 1024
+            collective_id=0, has_side_effects=True, vmem_limit_bytes=48 * 1024 * 1024
         ),
         name="minp",
-    )(states, head.T)
+    )(
+        pltpu.with_memory_space_constraint(states, pltpu.HBM),
+        pltpu.with_memory_space_constraint(head.T, pltpu.HBM),
+    )
     return jnp.maximum(gated - lnt, -logp_floor).T
 
 

time: 76.9 us -> 73.9 us (0.961)
  other arithmetic: 3.03 us -> 1.45 us
  Pallas kernels: 73.8 us -> 72.4 us
    transpose x1, other arithmetic: 3.03 us -> 1.45 us  [body(): return jnp.maximum(gated - lnt, -logp_floor).T]
    pallas_call x1, Pallas kernels: 73.8 us -> 72.4 us  [body(): pl.pallas_call(kernel, out_shape=(jax.ShapeDtypeStruct((COLS, OWNED), f32...]
where the time goes in v4:
time: 73.9 us; the launch traced here: 73.8 us
  Pallas kernels  72.4 us (98%)
  other arithmetic  1.45 us (2%)
    pallas_call x1, Pallas kernels, body(): pl.pallas_call(kernel, out_shape=(jax.ShapeDtypeStruct((COLS, OWNED), f32...  72.4 us

profile of v4, /device:TPU:1, one launch (start us, length us, event | category | flops | bytes accessed | tf_op | source)
XLA Modules:
  0.0 73.8 jit_solution(4569380668394374839)
XLA Ops:
  0.0 72.4 %minp.1 = (f32[2020,256]{1,0:T(8,128)S(1)}, f32[1,256]{1,0:T(1,128)S(1)}) custom-call(bf16[4,7168]{1,0:T(4,128)(2,1)} %states.1, bf16[2020,1792]{1,0:T(8,128)(2,1)} %bitcast.5), custom_call_target="tpu_custom_call" | custom-call | tf_op jit(solution)/shard_map/minp/pallas_call | solution.py:337
  72.4 1.4 %maximum_bitcast_fusion = f32[256,2020]{0,1:T(8,128)} fusion(f32[2020,256]{1,0:T(8,128)S(1)} %get-tuple-element.7, f32[256]{0:T(256)S(1)} %bitcast.4), kind=kLoop, calls=%fused_computation | loop fusion | flops 1034240 | bytes 4137984 | tf_op jit(solution)/shard_map/transpose | solution.py:378

commit v5 on v4

--- a/solution.py
+++ b/solution.py
@@ -32,8 +32,12 @@
 
 PLANE = [(dy, dx) for dy in range(NY) for dx in range(NX)]
 PLANE.sort(key=lambda p: -(min(p[0], NY - p[0]) + min(p[1], NX - p[1])))
-FAR = [(dy, dz) for dy in range(NY) for dz in range(NZ) if dy or dz]
-FAR.sort(key=lambda p: -(min(p[0], NY - p[0]) + min(p[1], NZ - p[1])))
+CHIPS = [(dy, dz) for dy in range(NY) for dz in range(NZ) if dy or dz]
+AWAY = {p: min(p[0], NY - p[0]) + min(p[1], NZ - p[1]) for p in CHIPS}
+CHIPS.sort(key=lambda p: -AWAY[p])
+FAR = [p for p in CHIPS if AWAY[p] >= 5]
+NEAR = [p for p in CHIPS if AWAY[p] < 5]
+LANDED = 2 * len(FAR) + len(NEAR)
 
 
 def coded(v):
@@ -62,9 +66,9 @@
 
 def kernel(
     states, head, gated, lnt_out,
-    raw, weights, xin, st, prod, s1out, s1in, s2out, s2in, acc, logits_t, col, exc, exn,
+    raw, weights, xin, st, prod, s1out, s1in, s2out, s2in, acc, logits_t, e4, e5, col, ex,
     w_sem, xl_sem, xs_sem, xr_sem, zs_sem, zr_sem, cs_sem, cr_sem,
-    s1s_sem, s1r_sem, s2s_sem, s2r_sem, ecs_sem, ecr_sem, ens_sem, enr_sem,
+    s1s_sem, s1r_sem, s2s_sem, s2r_sem, es_sem, er_sem,
 ):
     x, y, z, c = (lax.axis_index(n) for n in ("x", "y", "z", "c"))
 
@@ -166,9 +170,9 @@
             at(dx=1 if h == 0 else NX - 1),
         )
 
-    def second_hop(b, h):
+    def second_hop(b, h, part):
         return remote(
-            s2out.at[b, h], s2in.at[b, h], s2s_sem.at[b, h], s2r_sem.at[b, h],
+            s2out.at[b, h, part], s2in.at[b, h, part], s2s_sem.at[b, h, part], s2r_sem.at[b, h, part],
             at(dx=1 if h == 0 else NX - 1),
         )
 
@@ -186,37 +190,36 @@
             for lo, n in CHUNKS:
                 s1out[b, h, :, lo:lo + n] = coded(prod[b, rows_for(h, across), lo:lo + n])
             first_hop(b, h).start()
-
-    def relay(b):
         for h in (0, 1):
             to = right if h == 0 else left
             for lo, n in CHUNKS:
-                s2out[b, h, 16 * (1 - h):16 * (1 - h) + 16, lo:lo + n] = coded(
-                    prod[b, rows_for(1 - h, to), lo:lo + n]
-                )
+                s2out[b, h, 0, :, lo:lo + n] = coded(prod[b, rows_for(1 - h, to), lo:lo + n])
+            second_hop(b, h, 0).start()
+
+    def relay(b):
         for h in (0, 1):
             to = right if h == 0 else left
             first_hop(b, h).wait_recv()
             for lo, n in CHUNKS:
-                s2out[b, h, 16 * h:16 * h + 16, lo:lo + n] = coded(
+                s2out[b, h, 1, :, lo:lo + n] = coded(
                     prod[b, rows_for(h, to), lo:lo + n] + decoded(s1in[b, h, :, lo:lo + n])
                 )
-            second_hop(b, h).start()
+            second_hop(b, h, 1).start()
 
     def collect(b):
         alone = jnp.logical_or(b == 0, b == NZ - 1)
         s = (b + 1) // 2
-        second_hop(b, 0).wait_recv()
-        second_hop(b, 1).wait_recv()
-        for h in (0, 1):
-            rows = slice(16 * h, 16 * h + 16)
+        for h in (0, 1):
+            second_hop(b, 1 - h, 0).wait_recv()
+            second_hop(b, h, 1).wait_recv()
             block = jnp.where(alone, z + s, z + NZ + (2 * h - 1) * s) % NZ
             core = jnp.where(alone, h, 1 - b % 2)
             mine = pl.ds(pl.multiple_of(core * PIECE, PIECE), PIECE)
             best = None
             for lo, n in CHUNKS:
                 logits = prod[b, rows_for(h, x), lo:lo + n] + (
-                    decoded(s2in[b, 0, rows, lo:lo + n]) + decoded(s2in[b, 1, rows, lo:lo + n])
+                    decoded(s2in[b, h, 1, :, lo:lo + n])
+                    + decoded(s2in[b, 1 - h, 0, :, lo:lo + n])
                 )
                 acc[block, mine, lo:lo + n] = logits
                 part = lane_max(logits)
@@ -247,27 +250,38 @@
 
     lax.fori_loop(0, NZ + 3, step, 0)
 
+    best = jnp.max(jnp.transpose(col[...].reshape(OWNED, 128)), axis=0, keepdims=True)
+
     def exchanged(phase, row, combine, meanwhile):
-        exc[phase, 0] = row
+        ex[phase, 0] = row
+
+        def sent(source, target, device):
+            return remote(
+                ex.at[phase, source], ex.at[phase, target],
+                es_sem.at[phase, 1], er_sem.at[phase, 1], device,
+            )
+
         sibling = remote(
-            exc.at[phase, 0], exc.at[phase, 1], ecs_sem.at[phase], ecr_sem.at[phase], at(dc=1)
+            ex.at[phase, 0], ex.at[phase, 1], es_sem.at[phase, 0], er_sem.at[phase, 0], at(dc=1)
         )
         sibling.start()
+        for k, (dy, dz) in enumerate(FAR):
+            for dc in (0, 1):
+                sent(0, 3 + 2 * k + dc, at(dy=dy, dz=dz, dc=dc)).start()
         sibling.wait_recv()
-        exn[phase, 0] = combine(row, exc[phase, 1])
-        for k, (dy, dz) in enumerate(FAR):
-            remote(
-                exn.at[phase, 0], exn.at[phase, k + 1], ens_sem.at[phase], enr_sem.at[phase],
-                at(dy=dy, dz=dz),
-            ).start()
+        ex[phase, 2] = combine(row, ex[phase, 1])
+        for k, (dy, dz) in enumerate(NEAR):
+            sent(2, 3 + 2 * len(FAR) + k, at(dy=dy, dz=dz)).start()
         meanwhile()
-        arrived = exn.at[phase, pl.ds(1, len(FAR))]
-        everyone = remote(arrived, arrived, ens_sem.at[phase], enr_sem.at[phase], at(dz=1))
+        arrived = ex.at[phase, pl.ds(3, LANDED)]
+        everyone = remote(
+            arrived, arrived, es_sem.at[phase, 1], er_sem.at[phase, 1], at(dz=1)
+        )
         sibling.wait_send()
         everyone.wait_recv()
-        row = exn[phase, 0]
-        for k in range(len(FAR)):
-            row = combine(row, exn[phase, k + 1])
+        row = ex[phase, 2]
+        for k in range(LANDED):
+            row = combine(row, ex[phase, 3 + k])
         return row, everyone
 
     def settle(b, carry):
@@ -275,7 +289,8 @@
             pl.when(b >= 1)(along_z(b, h, b, h, h).wait_send)
             to_sibling(b, h).wait_send()
             first_hop(b, h).wait_send()
-            second_hop(b, h).wait_send()
+            second_hop(b, h, 0).wait_send()
+            second_hop(b, h, 1).wait_send()
         return carry
 
     def transposed():
@@ -289,25 +304,32 @@
             for lo in range(0, COLS, 128):
                 n = min(128, COLS - lo)
                 tile = acc[4 * g:4 * g + 4, :, lo:lo + n].reshape(128, n)
-                logits_t[lo:lo + n, 128 * g:128 * g + 128] = jnp.transpose(tile)
-
-    best = jnp.max(jnp.transpose(col[...].reshape(OWNED, 128)), axis=0, keepdims=True)
+                lanes = slice(128 * g, 128 * g + 128)
+                tile = jnp.transpose(tile)
+                logits_t[lo:lo + n, lanes] = tile
+                a = jnp.exp(tile - best[:, lanes])
+                a4 = (a * a) * (a * a)
+                e4[lo:lo + n, lanes] = a4
+                e5[lo:lo + n, lanes] = a4 * a
+
     top, sent_top = exchanged(0, best, jnp.maximum, transposed)
 
     cut = math.exp(-sharpness * minp_offset)
 
-    def kept(v):
-        a = jnp.exp(v - top)
-        a4 = (a * a) * (a * a)
-        return (a4 * a) / (a4 + cut)
+    scale = jnp.exp(best - top)
+    scale4 = (scale * scale) * (scale * scale)
+    scale5 = scale4 * scale
+
+    def kept(rows):
+        return (e5[rows, :] * scale5) / (e4[rows, :] * scale4 + cut)
 
     def add_rows(k, total):
-        mass = kept(logits_t[pl.ds(pl.multiple_of(k * STEP, 8), STEP), :])
+        mass = kept(pl.ds(pl.multiple_of(k * STEP, 8), STEP))
         return total + jnp.sum(mass.reshape(STEP // 8, 8, OWNED), axis=0)
 
     total = lax.fori_loop(0, TAIL // STEP, add_rows, jnp.zeros((8, OWNED), jnp.float32))
     total = jnp.sum(total, axis=0, keepdims=True) + jnp.sum(
-        kept(logits_t[TAIL:COLS, :]), axis=0, keepdims=True
+        kept(slice(TAIL, COLS)), axis=0, keepdims=True
     )
 
     def filtered(v):
@@ -350,22 +372,22 @@
             pltpu.VMEM((NZ, BLOCK, COLS), f32),
             pltpu.VMEM((NZ, 2, PIECE, COLS), bf16),
             pltpu.VMEM((NZ, 2, PIECE, COLS), bf16),
-            pltpu.VMEM((NZ, 2, 2 * PIECE, COLS), bf16),
-            pltpu.VMEM((NZ, 2, 2 * PIECE, COLS), bf16),
+            pltpu.VMEM((NZ, 2, 2, PIECE, COLS), bf16),
+            pltpu.VMEM((NZ, 2, 2, PIECE, COLS), bf16),
             pltpu.VMEM((NZ, 32, COLS), f32),
             pltpu.VMEM((COLS, OWNED), f32),
+            pltpu.VMEM((COLS, OWNED), f32),
+            pltpu.VMEM((COLS, OWNED), f32),
             pltpu.VMEM((NZ, 32, 128), f32),
-            pltpu.VMEM((2, 2, 1, OWNED), f32),
-            pltpu.VMEM((2, len(FAR) + 1, 1, OWNED), f32),
+            pltpu.VMEM((2, 3 + LANDED, 1, OWNED), f32),
             dma,
             dma,
             dma((len(PLANE),)), dma((len(PLANE),)),
             dma((NZ, 2)), dma((NZ, 2)),
             dma((NZ, 2)), dma((NZ, 2)),
             dma((NZ, 2)), dma((NZ, 2)),
-            dma((NZ, 2)), dma((NZ, 2)),
-            dma((2,)), dma((2,)),
-            dma((2,)), dma((2,)),
+            dma((NZ, 2, 2)), dma((NZ, 2, 2)),
+            dma((2, 2)), dma((2, 2)),
         ],
         compiler_params=pltpu.CompilerParams(
             collective_id=0, has_side_effects=True, vmem_limit_bytes=48 * 1024 * 1024

time: 73.9 us -> 71.9 us (0.973)
  Pallas kernels: 72.4 us -> 70.4 us
    pallas_call x1, Pallas kernels: 72.4 us -> 70.4 us  [body(): pl.pallas_call(kernel, out_shape=(jax.ShapeDtypeStruct((COLS, OWNED), f32...]
where the time goes in v5:
time: 71.9 us
  Pallas kernels  70.4 us (98%)
  other arithmetic  1.45 us (2%)
    pallas_call x1, Pallas kernels, body(): pl.pallas_call(kernel, out_shape=(jax.ShapeDtypeStruct((COLS, OWNED), f32...  70.4 us
    transpose x1, other arithmetic, body(): return jnp.maximum(gated - lnt, -logp_floor).T  1.45 us

profile of v5, /device:TPU:1, one launch (start us, length us, event | category | flops | bytes accessed | tf_op | source)
XLA Modules:
  0.0 71.9 jit_solution(5435460192431010224)
XLA Ops:
  0.0 70.4 %minp.1 = (f32[2020,256]{1,0:T(8,128)S(1)}, f32[1,256]{1,0:T(1,128)S(1)}) custom-call(bf16[4,7168]{1,0:T(4,128)(2,1)} %states.1, bf16[2020,1792]{1,0:T(8,128)(2,1)} %bitcast.5), custom_call_target="tpu_custom_call" | custom-call | tf_op jit(solution)/shard_map/minp/pallas_call | solution.py:359
  70.4 1.4 %maximum_bitcast_fusion = f32[256,2020]{0,1:T(8,128)} fusion(f32[2020,256]{1,0:T(8,128)S(1)} %get-tuple-element.7, f32[256]{0:T(256)S(1)} %bitcast.4), kind=kLoop, calls=%fused_computation | loop fusion | flops 1034240 | bytes 4137984 | tf_op jit(solution)/shard_map/transpose | solution.py:400

commit v6 on v5

--- a/solution.py
+++ b/solution.py
@@ -29,6 +29,7 @@
 POWER = 7
 STEP = 224
 TAIL = 9 * STEP
+BANDS = ((0, 256), (256, 512), (768, 512), (1280, 740))
 
 PLANE = [(dy, dx) for dy in range(NY) for dx in range(NX)]
 PLANE.sort(key=lambda p: -(min(p[0], NY - p[0]) + min(p[1], NX - p[1])))
@@ -66,8 +67,8 @@
 
 def kernel(
     states, head, gated, lnt_out,
-    raw, weights, xin, st, prod, s1out, s1in, s2out, s2in, acc, logits_t, e4, e5, col, ex,
-    w_sem, xl_sem, xs_sem, xr_sem, zs_sem, zr_sem, cs_sem, cr_sem,
+    staged, raw, weights, xin, st, prod, s1out, s1in, s2out, s2in, acc, logits_t, e4, e5, col, ex,
+    s_sem, w_sem, xl_sem, xs_sem, xr_sem, zs_sem, zr_sem, cs_sem, cr_sem,
     s1s_sem, s1r_sem, s2s_sem, s2r_sem, es_sem, er_sem,
 ):
     x, y, z, c = (lax.axis_index(n) for n in ("x", "y", "z", "c"))
@@ -86,6 +87,8 @@
             device_id=device, device_id_type=MESH,
         )
 
+    s_copy = pltpu.make_async_copy(states, staged, s_sem)
+    s_copy.start()
     w_copy = pltpu.make_async_copy(head, raw, w_sem)
     w_copy.start()
     keeper = y // 2
@@ -109,17 +112,18 @@
                         greet(sender)
     for device in (at(dz=1), at(dz=NZ - 1), at(dc=1)):
         greet(device)
+    s_copy.wait()
     pl.semaphore_wait(barrier, 19 - stays.astype(jnp.int32))
 
     def piece(k, dy, dx):
         to = (x + dx) % NX
         return remote(
-            states.at[:, pl.ds(pl.multiple_of(to * DEPTH, 128), DEPTH)], xin.at[slot],
+            staged.at[:, pl.ds(pl.multiple_of(to * DEPTH, 128), DEPTH)], xin.at[slot],
             xs_sem.at[k], xr_sem.at[slot], ((y + dy) % NY, z, keeper, to),
         )
 
     own_piece = pltpu.make_async_copy(
-        states.at[:, pl.ds(pl.multiple_of(x * DEPTH, 128), DEPTH)], xin.at[slot], xl_sem
+        staged.at[:, pl.ds(pl.multiple_of(x * DEPTH, 128), DEPTH)], xin.at[slot], xl_sem
     )
     for k, (dy, dx) in enumerate(PLANE):
         if dy or dx:
@@ -158,9 +162,8 @@
 
     for h in (0, 1):
         to_sibling(0, h).start()
-    for p in (0, 1):
-        for way in (0, 1):
-            along_z(0, p, 1 + p, way, way).start()
+    for way in (0, 1):
+        along_z(0, 0, 1, way, way).start()
 
     right, left, across = (x + 1) % NX, (x + NX - 1) % NX, (x + 2) % NX
 
@@ -243,6 +246,12 @@
 
     def step(b, carry):
         pl.when(b < NZ)(lambda: multiply(b))
+
+        @pl.when(b == 0)
+        def _():
+            for way in (0, 1):
+                along_z(0, 1, 2, way, way).start()
+
         pl.when(b < NZ - 1)(lambda: pass_on(b + 1))
         pl.when(jnp.logical_and(b != 1, b <= NZ))(lambda: relay(jnp.maximum(b - 1, 0)))
         pl.when(b >= 3)(lambda: collect(b - 3))
@@ -353,6 +362,18 @@
     sent_total.wait_send()
 
 
+def floored(gated, lnt, out, result, sems):
+    copies = []
+    for k, (lo, n) in enumerate(BANDS):
+        result[lo:lo + n, :] = jnp.maximum(gated[lo:lo + n, :] - lnt[...], -logp_floor)
+        copies.append(
+            pltpu.make_async_copy(result.at[lo:lo + n, :], out.at[lo:lo + n, :], sems.at[k])
+        )
+        copies[-1].start()
+    for copy in copies:
+        copy.wait()
+
+
 def body(states, head):
     dma = pltpu.SemaphoreType.DMA
     f32, bf16 = jnp.float32, jnp.bfloat16
@@ -365,6 +386,7 @@
         in_specs=[pl.BlockSpec(memory_space=pltpu.HBM)] * 2,
         out_specs=(pl.BlockSpec(memory_space=pltpu.VMEM),) * 2,
         scratch_shapes=[
+            pltpu.VMEM((LOCAL, NX * DEPTH), bf16),
             pltpu.VMEM((COLS, DEPTH), bf16),
             pltpu.VMEM((DEPTH, COLS), bf16),
             pltpu.VMEM((NY * NX, LOCAL, DEPTH), bf16),
@@ -382,6 +404,7 @@
             pltpu.VMEM((2, 3 + LANDED, 1, OWNED), f32),
             dma,
             dma,
+            dma,
             dma((len(PLANE),)), dma((len(PLANE),)),
             dma((NZ, 2)), dma((NZ, 2)),
             dma((NZ, 2)), dma((NZ, 2)),
@@ -397,7 +420,15 @@
         pltpu.with_memory_space_constraint(states, pltpu.HBM),
         pltpu.with_memory_space_constraint(head.T, pltpu.HBM),
     )
-    return jnp.maximum(gated - lnt, -logp_floor).T
+    return pl.pallas_call(
+        floored,
+        out_shape=jax.ShapeDtypeStruct((COLS, OWNED), f32),
+        in_specs=[pl.BlockSpec(memory_space=pltpu.VMEM)] * 2,
+        out_specs=pl.BlockSpec(memory_space=pl.ANY),
+        scratch_shapes=[pltpu.VMEM((COLS, OWNED), f32), dma((len(BANDS),))],
+        compiler_params=pltpu.CompilerParams(vmem_limit_bytes=8 * 1024 * 1024),
+        name="floored",
+    )(gated, lnt).T
 
 
 def solution(mesh):

time: 71.9 us -> 70.7 us (0.983)
  other arithmetic: 1.45 us -> 0 us
    transpose x1 -> x0, other arithmetic: 1.45 us -> none  [body(): return jnp.maximum(gated - lnt, -logp_floor).T]
    pallas_call x0 -> x1, Pallas kernels: none -> 1.36 us  [body(): pl.pallas_call(floored, out_shape=jax.ShapeDtypeStruct((COLS, OWNED), f32...]
    pallas_call x1, Pallas kernels: 70.4 us -> 69.2 us  [body(): pl.pallas_call(kernel, out_shape=(jax.ShapeDtypeStruct((COLS, OWNED), f32...]
where the time goes in v6:
time: 70.7 us; the launch traced here: 70.6 us
  Pallas kernels  70.6 us (100%)
    pallas_call x1, Pallas kernels, body(): pl.pallas_call(kernel, out_shape=(jax.ShapeDtypeStruct((COLS, OWNED), f32...  69.2 us

profile of v6, /device:TPU:1, one launch (start us, length us, event | category | flops | bytes accessed | tf_op | source)
XLA Modules:
  0.0 70.6 jit_solution(11965924711677864226)
XLA Ops:
  0.0 69.2 %minp.1 = (f32[2020,256]{1,0:T(8,128)S(1)}, f32[1,256]{1,0:T(1,128)S(1)}) custom-call(bf16[4,7168]{1,0:T(4,128)(2,1)} %states.1, bf16[2020,1792]{1,0:T(8,128)(2,1)} %bitcast.2), custom_call_target="tpu_custom_call" | custom-call | tf_op jit(solution)/shard_map/minp/pallas_call | solution.py:380
  69.3 1.4 %floored.1 = f32[2020,256]{1,0:T(8,128)} custom-call(f32[2020,256]{1,0:T(8,128)S(1)} %get-tuple-element.7.gated, f32[1,256]{1,0:T(1,128)S(1)} %get-tuple-element.8.lnt), custom_call_target="tpu_custom_call" | custom-call | tf_op jit(solution)/shard_map/floored/pallas_call | solution.py:423

commit v7 on v6

--- a/solution.py
+++ b/solution.py
@@ -100,7 +100,7 @@
     def greet(device):
         pl.semaphore_signal(barrier, inc=1, device_id=device, device_id_type=MESH)
 
-    for dx in range(NX):
+    for dx in (2, 1, 3, 0):
         for j in range(2):
             for cc in range(NC):
                 sender = (2 * c + j, z, cc, (x + dx) % NX)
@@ -160,10 +160,10 @@
     def to_sibling(b, h):
         return remote(share(b, h), share(b, h), cs_sem.at[b, h], cr_sem.at[b, h], at(dc=1))
 
+    for way in (0, 1):
+        along_z(0, 0, 1, way, way).start()
     for h in (0, 1):
         to_sibling(0, h).start()
-    for way in (0, 1):
-        along_z(0, 0, 1, way, way).start()
 
     right, left, across = (x + 1) % NX, (x + NX - 1) % NX, (x + 2) % NX
 

time: 70.7 us -> 70.7 us (level)
  no operation moved by 1% of the time
where the time goes in v7:
time: 70.7 us; the launch traced here: 70.6 us
  Pallas kernels  70.6 us (100%)
    pallas_call x1, Pallas kernels, body(): pl.pallas_call(kernel, out_shape=(jax.ShapeDtypeStruct((COLS, OWNED), f32...  69.2 us

profile of v7, /device:TPU:1, one launch (start us, length us, event | category | flops | bytes accessed | tf_op | source)
XLA Modules:
  0.0 70.6 jit_solution(4455884130709521373)
XLA Ops:
  0.0 69.2 %minp.1 = (f32[2020,256]{1,0:T(8,128)S(1)}, f32[1,256]{1,0:T(1,128)S(1)}) custom-call(bf16[4,7168]{1,0:T(4,128)(2,1)} %states.1, bf16[2020,1792]{1,0:T(8,128)(2,1)} %bitcast.2), custom_call_target="tpu_custom_call" | custom-call | tf_op jit(solution)/shard_map/minp/pallas_call | solution.py:380
  69.2 1.4 %floored.1 = f32[2020,256]{1,0:T(8,128)} custom-call(f32[2020,256]{1,0:T(8,128)S(1)} %get-tuple-element.7.gated, f32[1,256]{1,0:T(1,128)S(1)} %get-tuple-element.8.lnt), custom_call_target="tpu_custom_call" | custom-call | tf_op jit(solution)/shard_map/floored/pallas_call | solution.py:423

commit v8 on v7

--- a/solution.py
+++ b/solution.py
@@ -36,8 +36,8 @@
 CHIPS = [(dy, dz) for dy in range(NY) for dz in range(NZ) if dy or dz]
 AWAY = {p: min(p[0], NY - p[0]) + min(p[1], NZ - p[1]) for p in CHIPS}
 CHIPS.sort(key=lambda p: -AWAY[p])
-FAR = [p for p in CHIPS if AWAY[p] >= 5]
-NEAR = [p for p in CHIPS if AWAY[p] < 5]
+FAR = [p for p in CHIPS if AWAY[p] >= 4]
+NEAR = [p for p in CHIPS if AWAY[p] < 4]
 LANDED = 2 * len(FAR) + len(NEAR)
 
 
@@ -330,7 +330,7 @@
     scale5 = scale4 * scale
 
     def kept(rows):
-        return (e5[rows, :] * scale5) / (e4[rows, :] * scale4 + cut)
+        return e5[rows, :] / (e4[rows, :] * scale4 + cut)
 
     def add_rows(k, total):
         mass = kept(pl.ds(pl.multiple_of(k * STEP, 8), STEP))
@@ -340,6 +340,7 @@
     total = jnp.sum(total, axis=0, keepdims=True) + jnp.sum(
         kept(slice(TAIL, COLS)), axis=0, keepdims=True
     )
+    total = total * scale5
 
     def filtered(v):
         shifted = v - top

time: 70.7 us -> 70.6 us (level)
  no operation moved by 1% of the time
where the time goes in v8:
time: 70.6 us; the launch traced here: 70.5 us
  Pallas kernels  70.5 us (100%)
    pallas_call x1, Pallas kernels, body(): pl.pallas_call(kernel, out_shape=(jax.ShapeDtypeStruct((COLS, OWNED), f32...  69.1 us

profile of v8, /device:TPU:1, one launch (start us, length us, event | category | flops | bytes accessed | tf_op | source)
XLA Modules:
  0.0 70.5 jit_solution(11350591071593806993)
XLA Ops:
  0.0 69.1 %minp.1 = (f32[2020,256]{1,0:T(8,128)S(1)}, f32[1,256]{1,0:T(1,128)S(1)}) custom-call(bf16[4,7168]{1,0:T(4,128)(2,1)} %states.1, bf16[2020,1792]{1,0:T(8,128)(2,1)} %bitcast.2), custom_call_target="tpu_custom_call" | custom-call | tf_op jit(solution)/shard_map/minp/pallas_call | solution.py:381
  69.1 1.4 %floored.1 = f32[2020,256]{1,0:T(8,128)} custom-call(f32[2020,256]{1,0:T(8,128)S(1)} %get-tuple-element.7.gated, f32[1,256]{1,0:T(1,128)S(1)} %get-tuple-element.8.lnt), custom_call_target="tpu_custom_call" | custom-call | tf_op jit(solution)/shard_map/floored/pallas_call | solution.py:424
